TPU v7x, 512 devices: a whole 4x8x8 slice. The times are simulated.
512 devices in a mesh: row: 16 (over y, x_hi), col: 32 (over z, x_lo, core).
Axes of the slice: x: 4 (x_hi: 2, x_lo: 2; x = x_hi * 2 + x_lo), y: 8, z: 8, core: 2. Of those that a mesh axis runs over, the one named last changes fastest.
Arguments:
- sigma_anc: bfloat16 [4096, 4096], P('row', 'col'), as said below
- structure: int32 [512, 4], P(('row', 'col')), may hold values from 0 to 15, all different within a row
- factor: bfloat16 [512, 1024, 1024], P(('row', 'col')), may hold values from -0.375 to 0.375
- diag_term: float32 [512, 1024], P(('row', 'col')), may hold values from 1 to 8
Outputs:
- sigma_off: bfloat16 [512, 1024, 1024], P(('row', 'col'))
- variances: float32 [512, 1024], P(('row', 'col'))
Inputs may be any that keep to these rules, and one draw needn't show every extreme that they name: `structure`: each row names 4 different ancestor blocks, and every ancestor block is named by some row. sigma_anc is exactly symmetric, as the inverse of a symmetric precision matrix: its entry (p, q) equals its entry (q, p) bit for bit.
All inputs are finite; a program needn't handle non-finite values.
Results may differ from a plain program's by a relative error of at most 0.001.
Values may be sent and summed in bfloat16 or wider, within the bound.
No kernel may reach another device: no remote copies, remote signals or barrier semaphores. Data moves between devices by JAX's collectives and lax.ppermute only.
A program may use at most 64 MiB of HBM per device.

v0:
```python
import jax
import jax.numpy as jnp
from jax import lax
from jax.sharding import PartitionSpec as P


def body(sigma_anc, structure, factor, diag_term):
    span_count = structure.shape[1]
    block_rows = factor.shape[1] // span_count
    own_blocks = structure[0]
    triangle = factor[0]
    panel = lax.all_gather(sigma_anc, "col", axis=1, tiled=True)
    structures = lax.all_gather(structure, "row", axis=0, tiled=True)
    block_total = panel.shape[1] // block_rows
    blocked = panel.reshape(block_rows, block_total, block_rows)
    outgoing = jnp.take(blocked, structures, axis=1)
    outgoing = outgoing.reshape(block_rows, structures.shape[0], span_count * block_rows)
    received = lax.all_to_all(outgoing, "row", split_axis=1, concat_axis=1, tiled=True)
    picked = jnp.take(received, own_blocks, axis=1)
    product = jnp.einsum("bim,mw->ibw", picked, triangle, preferred_element_type=jnp.float32)
    off_block = -product.reshape(span_count * block_rows, triangle.shape[1])
    variance = diag_term[0] - jnp.sum(triangle.astype(jnp.float32) * off_block, axis=0)
    return (off_block.astype(jnp.bfloat16)[None], variance[None])


def solution(mesh):
    return jax.shard_map(
        body,
        mesh=mesh,
        in_specs=(
            P("row", "col"),
            P(("row", "col"), None),
            P(("row", "col"), None, None),
            P(("row", "col"), None),
        ),
        out_specs=(P(("row", "col"), None, None), P(("row", "col"), None)),
        check_vma=False,
    )
```

profile of v0, /device:TPU:17, one launch (start us, length us, event | category | flops | bytes accessed | tf_op | source)
XLA Modules:
  0.0 328.1 jit_solution(7711862939301773111)
XLA Ops:
  7.2 0.0 all-gather.3.cloned.1.call-start
  7.2 1.6 copy.21
  8.8 0.0 all-gather.3.cloned.1.call-update
  8.8 30.0 %all-gather = s32[16,1,4]{2,1,0:T(1,128)S(1)} all-gather(s32[1,1,4]{2,1,0:T(1,128)} %bitcast.47), channel_id=1, replica_groups=mesh['row'=16,'col'=32] {'row'}, dimensions={0}, use_global_device_ids=true | all-gather | bytes 272 | tf_op jit(solution)/shard_map/all_gather | solution.py:13
  38.8 0.1 copy.19
  38.9 0.1 copy.22
  39.0 0.1 reshape.70
  39.1 0.1 copy.20
  39.2 0.1 broadcast_in_dim.29
  39.3 43.8 %all-gather.3.cloned.1.call-done = bf16[256,4096]{0,1:T(8,128)(2,1)} async-done(((bf16[256,128]{0,1:T(8,128)(2,1)}), bf16[256,4096]{0,1:T(8,128)(2,1)}) %all-gather.3.cloned.1.call-update) | async-done | bytes 2097168 | tf_op jit(solution)/shard_map/all_gather | solution.py:12
  83.1 2.8 copy.23
  86.0 5.5 %gather_fusion = bf16[64,256,256]{2,1,0:T(8,128)(2,1)} fusion(bf16[256,16,256]{2,0,1:T(8,128)(2,1)S(1)} %copy.23, s32[1024]{0:T(1024)S(1)} %pad_clamp_fusion.1), kind=kCustom, calls=%fused_computation | custom fusion | bytes 16777472 | tf_op jit(solution)/shard_map/jit(_take)/gather | solution.py:16
  91.5 7.7 %copy.25 = bf16[16,4,32,8,256]{4,3,1,2,0:T(8,128)(2,1)} copy(bf16[16,4,32,8,256]{4,3,2,1,0:T(8,128)(2,1)} %bitcast.42) | data formatting | bytes 16777216 | tf_op jit(solution)/shard_map/jit(_take)/gather | solution.py:16
  99.1 7.4 %broadcast_select_fusion = bf16[256,16,1024]{2,0,1:T(8,128)(2,1)} fusion(bf16[256,16,1024]{2,0,1:T(8,128)(2,1)} %bitcast.41, pred[16,1024]{1,0:T(8,128)(4,1)S(1)} %bitcast.44), kind=kLoop, calls=%fused_computation.2 | loop fusion | flops 4194304 | bytes 16793600 | tf_op jit(solution)/shard_map/jit(_take)/select_n | solution.py:16
  106.5 0.0 copy-start.2
  106.5 9.0 %all-to-all-start = ((bf16[256,16,1024]{2,0,1:T(8,128)(2,1)}), bf16[256,16,1024]{2,0,1:T(8,128)(2,1)}, u32[]{:S(2)}, u32[]{:S(2)}) async-start(bf16[256,16,1024]{2,0,1:T(8,128)(2,1)} %broadcast_select_fusion), calls=%async_computation | async-start | bytes 16777216 | tf_op jit(solution)/shard_map/all_to_all | solution.py:18
  115.5 0.0 copy-done.2
  115.6 194.9 %all-to-all-done = bf16[256,16,1024]{2,0,1:T(8,128)(2,1)} async-done(((bf16[256,16,1024]{2,0,1:T(8,128)(2,1)}), bf16[256,16,1024]{2,0,1:T(8,128)(2,1)}, u32[]{:S(2)}, u32[]{:S(2)}) %all-to-all-start) | async-done | bytes 8388640 | tf_op jit(solution)/shard_map/all_to_all | solution.py:18
  310.4 4.1 %gather_fusion.1 = bf16[4,256,1024]{2,1,0:T(8,128)(2,1)S(1)} fusion(bf16[256,16,1024]{2,0,1:T(8,128)(2,1)} %all-to-all-done, s32[1024]{0:T(1024)S(1)} %pad_clamp_fusion), kind=kCustom, calls=%fused_computation.1 | custom fusion | bytes 4194320 | tf_op jit(solution)/shard_map/jit(_take)/gather | solution.py:19
  314.5 0.0 copy-start
  314.5 5.4 %fusion.8 = (bf16[256,4,1024]{2,0,1:T(8,128)(2,1)}, f32[256,4,1024]{2,0,1:T(8,128)S(1)}) fusion(bf16[1,1024,1024]{2,1,0:T(8,128)(2,1)} %param.6, bf16[4,256,1024]{2,1,0:T(8,128)(2,1)S(1)} %gather_fusion.1, pred[4]{0:T(512)(128)(4,1)S(1)} %compare_and_fusion.1), kind=kOutput, calls=%fused_computation.20 | convolution fusion | flops 2150629376 | bytes 10485764 | tf_op jit(solution)/shard_map/bim,mw->ibw/dot_general | solution.py:20
  319.9 0.0 copy-done
  319.9 0.0 copy-start.1
  319.9 0.5 fusion
  320.5 0.1 copy-done.1
  320.6 0.6 sub.4
  (7 shorter events, 0.0 us)
Async XLA Ops:
  7.2 75.9 %all-gather.3.cloned.1.call-start = ((), (), s32[]{:S(2)}) async-start(), calls=%async_computation.1 | async-start | bytes 2162688 | tf_op jit(solution)/shard_map/all_gather | solution.py:12
  106.5 9.0 %copy-start.2 = (s32[1,4]{1,0:T(1,128)S(1)}, s32[1,4]{1,0:T(1,128)}, u32[]{:S(2)}) copy-start(s32[1,4]{1,0:T(1,128)} %param.5) | copy-start | bytes 52
  106.5 203.9 %all-to-all-start = ((bf16[256,16,1024]{2,0,1:T(8,128)(2,1)}), bf16[256,16,1024]{2,0,1:T(8,128)(2,1)}, u32[]{:S(2)}, u32[]{:S(2)}) async-start(bf16[256,16,1024]{2,0,1:T(8,128)(2,1)} %broadcast_select_fusion), calls=%async_computation | async-start | bytes 16777216 | tf_op jit(solution)/shard_map/all_to_all | solution.py:18
  314.5 5.4 %copy-start = (bf16[1,1024,1024]{2,1,0:T(8,128)(2,1)S(1)}, bf16[1,1024,1024]{2,1,0:T(8,128)(2,1)}, u32[]{:S(2)}) copy-start(bf16[1,1024,1024]{2,1,0:T(8,128)(2,1)} %param.6) | copy-start | bytes 6291460
  319.9 0.7 copy-start.1
Sparse Core Ops, SparseCore 0:
  10.7 72.3 all-gather.2
where the time goes:
time: 329 us; the launch traced here: 328 us
  waiting for transfers between devices  239 us (73%)
  blocking collectives  30 us (9%)
  local copies, waits for them, and re-layouts  22.3 us (7%)
  between operations  14.1 us (4%)
  starting transfers between devices  9.01 us (3%)
  other arithmetic  8.57 us (3%)
  matrix products  5.43 us (2%)
    all_to_all x1, waiting for transfers between devices, body(): lax.all_to_all(outgoing, 'row', split_axis=1, concat_axis=1, tiled=True)  195 us
    all_gather x1, waiting for transfers between devices, body(): panel = lax.all_gather(sigma_anc, 'col', axis=1, tiled=True)  43.8 us
    all_gather x1, blocking collectives, body(): structures = lax.all_gather(structure, 'row', axis=0, tiled=True)  30 us
    gather x2, local copies, waits for them, and re-layouts, body(): outgoing = jnp.take(blocked, structures, axis=1)  13.2 us
    all_to_all x1, starting transfers between devices, body(): lax.all_to_all(outgoing, 'row', split_axis=1, concat_axis=1, tiled=True)  8.97 us
    select_n x2, other arithmetic, body(): outgoing = jnp.take(blocked, structures, axis=1)  7.4 us
  transfers between devices with their start and end apart: 2, of which 2 were waited for; matrix products, arithmetic and copies ran while one was open for 0% of the time, Pallas kernels for 0%

commit v1 on v0

--- a/solution.py
+++ b/solution.py
@@ -9,7 +9,9 @@
     block_rows = factor.shape[1] // span_count
     own_blocks = structure[0]
     triangle = factor[0]
-    panel = lax.all_gather(sigma_anc, "col", axis=1, tiled=True)
+    panel = jnp.concatenate(
+        lax.all_to_all(jnp.stack([sigma_anc] * lax.axis_size("col")), "col", 0, 0), axis=1
+    )
     structures = lax.all_gather(structure, "row", axis=0, tiled=True)
     block_total = panel.shape[1] // block_rows
     blocked = panel.reshape(block_rows, block_total, block_rows)

time: 329 us -> 306 us (0.930)
  the two profiles are of different devices: /device:TPU:17 before, /device:TPU:23 now
where the time goes in v1:
time: 306 us; the launch traced here: 305 us
  waiting for transfers between devices  214 us (70%)
  blocking collectives  30.4 us (10%)
  local copies, waits for them, and re-layouts  24.6 us (8%)
  starting transfers between devices  21.6 us (7%)
  other arithmetic  8.57 us (3%)
  matrix products  5.43 us (2%)
    all_to_all x1, waiting for transfers between devices, body(): lax.all_to_all(outgoing, 'row', split_axis=1, concat_axis=1, tiled=True)  195 us
    all_gather x1, blocking collectives, body(): structures = lax.all_gather(structure, 'row', axis=0, tiled=True)  30.4 us
    all_to_all x1, waiting for transfers between devices, body(): lax.all_to_all(jnp.stack([sigma_anc] * lax.axis_size('col')), 'col', 0, 0)  19.2 us
    gather x2, local copies, waits for them, and re-layouts, body(): outgoing = jnp.take(blocked, structures, axis=1)  13.2 us
    all_to_all x1, starting transfers between devices, body(): lax.all_to_all(jnp.stack([sigma_anc] * lax.axis_size('col')), 'col', 0, 0)  12.3 us
    all_to_all x1, starting transfers between devices, body(): lax.all_to_all(outgoing, 'row', split_axis=1, concat_axis=1, tiled=True)  9.29 us
    select_n x2, other arithmetic, body(): outgoing = jnp.take(blocked, structures, axis=1)  7.4 us
  transfers between devices with their start and end apart: 2, of which 2 were waited for; matrix products, arithmetic and copies ran while one was open for 0% of the time, Pallas kernels for 0%

profile of v1, /device:TPU:23, one launch (start us, length us, event | category | flops | bytes accessed | tf_op | source)
XLA Modules:
  0.0 305.3 jit_solution(8509128801347750438)
XLA Ops:
  0.6 0.9 copy.17
  1.6 1.6 stack.2
  3.1 0.0 copy-start.3
  3.1 12.3 %all-to-all-start = ((bf16[32,256,128]{1,2,0:T(8,128)(2,1)}), bf16[32,256,128]{1,2,0:T(8,128)(2,1)S(1)}, u32[]{:S(2)}, u32[]{:S(2)}) async-start(bf16[32,256,128]{1,2,0:T(8,128)(2,1)} %stack.2), calls=%async_computation | async-start | bytes 4194304 | tf_op jit(solution)/shard_map/all_to_all | solution.py:13
  15.5 0.0 copy-done.3
  15.5 30.4 %all-gather = s32[16,1,4]{2,1,0:T(1,128)S(1)} all-gather(s32[1,1,4]{2,1,0:T(1,128)S(1)} %bitcast.49), channel_id=1, replica_groups=mesh['row'=16,'col'=32] {'row'}, dimensions={0}, use_global_device_ids=true | all-gather | bytes 272 | tf_op jit(solution)/shard_map/all_gather | solution.py:15
  45.8 0.1 copy.15
  45.9 0.1 copy.18
  46.0 0.1 reshape.72
  46.1 0.1 copy.16
  46.2 0.1 broadcast_in_dim.29
  46.4 19.2 %all-to-all-done = bf16[32,256,128]{1,2,0:T(8,128)(2,1)S(1)} async-done(((bf16[32,256,128]{1,2,0:T(8,128)(2,1)}), bf16[32,256,128]{1,2,0:T(8,128)(2,1)S(1)}, u32[]{:S(2)}, u32[]{:S(2)}) %all-to-all-start) | async-done | bytes 2097184 | tf_op jit(solution)/shard_map/all_to_all | solution.py:13
  65.6 0.0 copy-start
  65.6 1.3 copy-done
  66.9 2.8 copy.19
  69.8 5.5 %gather_fusion = bf16[64,256,256]{2,1,0:T(8,128)(2,1)} fusion(bf16[256,16,256]{2,0,1:T(8,128)(2,1)S(1)} %copy.19, s32[1024]{0:T(1024)S(1)} %pad_clamp_fusion.1), kind=kCustom, calls=%fused_computation | custom fusion | bytes 16777472 | tf_op jit(solution)/shard_map/jit(_take)/gather | solution.py:18
  75.3 7.7 %copy.21 = bf16[16,4,32,8,256]{4,3,1,2,0:T(8,128)(2,1)} copy(bf16[16,4,32,8,256]{4,3,2,1,0:T(8,128)(2,1)} %bitcast.44) | data formatting | bytes 16777216 | tf_op jit(solution)/shard_map/jit(_take)/gather | solution.py:18
  83.0 7.4 %broadcast_select_fusion = bf16[256,16,1024]{2,0,1:T(8,128)(2,1)} fusion(bf16[256,16,1024]{2,0,1:T(8,128)(2,1)} %bitcast.43, pred[16,1024]{1,0:T(8,128)(4,1)S(1)} %bitcast.46), kind=kLoop, calls=%fused_computation.2 | loop fusion | flops 4194304 | bytes 16793600 | tf_op jit(solution)/shard_map/jit(_take)/select_n | solution.py:18
  90.4 9.3 %all-to-all-start.1 = ((bf16[256,16,1024]{2,0,1:T(8,128)(2,1)}), bf16[256,16,1024]{2,0,1:T(8,128)(2,1)}, u32[]{:S(2)}, u32[]{:S(2)}) async-start(bf16[256,16,1024]{2,0,1:T(8,128)(2,1)} %broadcast_select_fusion), calls=%async_computation.1 | async-start | bytes 16777216 | tf_op jit(solution)/shard_map/all_to_all | solution.py:20
  99.7 194.8 %all-to-all-done.1 = bf16[256,16,1024]{2,0,1:T(8,128)(2,1)} async-done(((bf16[256,16,1024]{2,0,1:T(8,128)(2,1)}), bf16[256,16,1024]{2,0,1:T(8,128)(2,1)}, u32[]{:S(2)}, u32[]{:S(2)}) %all-to-all-start.1) | async-done | bytes 8388640 | tf_op jit(solution)/shard_map/all_to_all | solution.py:20
  294.5 4.1 %gather_fusion.1 = bf16[4,256,1024]{2,1,0:T(8,128)(2,1)S(1)} fusion(bf16[256,16,1024]{2,0,1:T(8,128)(2,1)} %all-to-all-done.1, s32[1024]{0:T(1024)S(1)} %pad_clamp_fusion), kind=kCustom, calls=%fused_computation.1 | custom fusion | bytes 4194320 | tf_op jit(solution)/shard_map/jit(_take)/gather | solution.py:21
  298.6 0.0 copy-start.1
  298.6 5.4 %fusion.8 = (bf16[256,4,1024]{2,0,1:T(8,128)(2,1)}, f32[256,4,1024]{2,0,1:T(8,128)S(1)}) fusion(bf16[1,1024,1024]{2,1,0:T(8,128)(2,1)} %param.6, bf16[4,256,1024]{2,1,0:T(8,128)(2,1)S(1)} %gather_fusion.1, pred[4]{0:T(512)(128)(4,1)S(1)} %compare_and_fusion.1), kind=kOutput, calls=%fused_computation.20 | convolution fusion | flops 2150629376 | bytes 10485764 | tf_op jit(solution)/shard_map/bim,mw->ibw/dot_general | solution.py:22
  304.0 0.0 copy-done.1
  304.0 0.0 copy-start.2
  304.0 0.5 fusion
  304.6 0.1 copy-done.2
  304.7 0.6 sub.4
  (7 shorter events, 0.0 us)
Async XLA Ops:
  3.1 12.4 %copy-start.3 = (s32[1,4]{1,0:T(1,128)S(1)}, s32[1,4]{1,0:T(1,128)}, u32[]{:S(2)}) copy-start(s32[1,4]{1,0:T(1,128)} %param.5) | copy-start | bytes 52
  3.1 62.5 %all-to-all-start = ((bf16[32,256,128]{1,2,0:T(8,128)(2,1)}), bf16[32,256,128]{1,2,0:T(8,128)(2,1)S(1)}, u32[]{:S(2)}, u32[]{:S(2)}) async-start(bf16[32,256,128]{1,2,0:T(8,128)(2,1)} %stack.2), calls=%async_computation | async-start | bytes 4194304 | tf_op jit(solution)/shard_map/all_to_all | solution.py:13
  65.6 1.3 copy-start
  90.4 204.1 %all-to-all-start.1 = ((bf16[256,16,1024]{2,0,1:T(8,128)(2,1)}), bf16[256,16,1024]{2,0,1:T(8,128)(2,1)}, u32[]{:S(2)}, u32[]{:S(2)}) async-start(bf16[256,16,1024]{2,0,1:T(8,128)(2,1)} %broadcast_select_fusion), calls=%async_computation.1 | async-start | bytes 16777216 | tf_op jit(solution)/shard_map/all_to_all | solution.py:20
  298.6 5.4 %copy-start.1 = (bf16[1,1024,1024]{2,1,0:T(8,128)(2,1)S(1)}, bf16[1,1024,1024]{2,1,0:T(8,128)(2,1)}, u32[]{:S(2)}) copy-start(bf16[1,1024,1024]{2,1,0:T(8,128)(2,1)} %param.6) | copy-start | bytes 6291460
  304.0 0.7 copy-start.2
